TPU v7x, 32 devices: a whole 2x2x4 slice. The times are simulated.
32 devices in a mesh: freq: 8 (over z, x), pair: 4 (over y, core).
Axes of the slice: x: 2, y: 2, z: 4, core: 2. Of those that a mesh axis runs over, the one named last changes fastest.
Arguments:
- samples: bfloat16 [2048, 8, 2, 1024], P(('freq', 'pair')), may hold values from -6 to 6
- rfi_flags: int32 [8, 1024], P('freq'), may hold values 0 or 1
- feed_map: int32 [2048], replicated, may hold values from 0 to 2047, each once
Outputs:
- visibilities: bfloat16 [8, 2, 2048, 2048], P('freq', None, 'pair')
Inputs may be any that keep to these rules, and one draw needn't show every extreme that they name: `feed_map`: each of the 2048 feeds is assigned to exactly one slot.
All inputs are finite; a program needn't handle non-finite values. No bound on the sum of `rfi_flags` on one device may be relied on, other than what follows from the above.
Results may differ from a plain program's by a relative error of at most 0.001.
Values may be sent and summed in bfloat16 or wider, within the bound.
No kernel may reach another device: no remote copies, remote signals or barrier semaphores. Data moves between devices by JAX's collectives and lax.ppermute only.
A program may use at most 64 MiB of HBM per device.

v0:
```python
import jax
import jax.numpy as jnp
from jax import lax
from jax.sharding import PartitionSpec as P


def local(samples, rfi_flags, feed_map):
    n_pair = lax.axis_size("pair")
    n_freq = lax.axis_size("freq")
    member = lax.axis_index("pair")
    keep_mask = (1 - rfi_flags).astype(jnp.bfloat16)
    shard_feeds = samples.shape[0]
    turned = lax.all_to_all(samples, "freq", split_axis=1, concat_axis=0, tiled=True)
    turned = turned * keep_mask[None, :, None, :]
    kept = lax.all_gather(turned, "pair", axis=0, tiled=True)
    shard_index = feed_map // shard_feeds
    within = feed_map % shard_feeds
    position = (
        shard_index % n_pair * (n_freq * shard_feeds) + shard_index // n_pair * shard_feeds + within
    )
    feed_count = kept.shape[0]
    steps_time = kept.shape[3]
    row_count = feed_count // n_pair
    inverse = 1.0 / steps_time
    feeds_all = kept[:, 0].reshape(feed_count, 2 * steps_time)
    columns = jnp.take(feeds_all, position, axis=0)
    own_rows = lax.dynamic_slice_in_dim(columns, member * row_count, row_count, 0)
    rotated_rows = jnp.concatenate([own_rows[:, steps_time:], -own_rows[:, :steps_time]], axis=1)
    stacked = jnp.concatenate([own_rows, rotated_rows], axis=0)
    product = lax.dot_general(
        stacked, columns, (((1,), (1,)), ((), ())), preferred_element_type=jnp.float32
    )
    results = [(product * inverse).astype(jnp.bfloat16).reshape(2, row_count, columns.shape[0])]
    computed = jnp.stack(results, axis=0)
    return computed


def solution(mesh):
    in_specs = (P(("freq", "pair"), None, None, None), P("freq", None), P())
    out_specs = P("freq", None, "pair", None)
    return jax.shard_map(local, mesh=mesh, in_specs=in_specs, out_specs=out_specs, check_vma=False)
```

profile of v0, /device:TPU:0, one launch (start us, length us, event | category | flops | bytes accessed | tf_op | source)
XLA Modules:
  0.0 202.3 jit_solution(14040332480941497455)
XLA Ops:
  6.5 0.0 copy-start.2
  6.5 4.1 %copy.6 = bf16[64,8,2,1024]{3,0,2,1:T(8,128)(2,1)} copy(bf16[64,8,2,1024]{3,2,1,0:T(2,128)(2,1)} %param.3) | data formatting | bytes 4194304 | tf_op args[0]
  10.6 0.0 copy-start.1
  10.6 7.4 %all-to-all-start = ((bf16[64,8,2,1024]{3,0,2,1:T(8,128)(2,1)}), bf16[64,8,2,1024]{3,0,2,1:T(8,128)(2,1)S(1)}, u32[]{:S(2)}, u32[]{:S(2)}) async-start(bf16[64,8,2,1024]{3,0,2,1:T(8,128)(2,1)} %copy.6), calls=%async_computation | async-start | bytes 4194304 | tf_op jit(solution)/shard_map/all_to_all | solution.py:13
  18.0 0.0 all-gather.2.cloned.1.call-start
  18.1 0.0 copy-done.2
  18.1 48.2 %all-to-all-done = bf16[64,8,2,1024]{3,0,2,1:T(8,128)(2,1)S(1)} async-done(((bf16[64,8,2,1024]{3,0,2,1:T(8,128)(2,1)}), bf16[64,8,2,1024]{3,0,2,1:T(8,128)(2,1)S(1)}, u32[]{:S(2)}, u32[]{:S(2)}) %all-to-all-start) | async-done | bytes 2097184 | tf_op jit(solution)/shard_map/all_to_all | solution.py:13
  66.3 0.2 copy.7
  66.4 1.6 bitcast_multiply_fusion
  68.0 0.0 all-gather.2.cloned.1.call-update
  68.1 0.0 copy-done.1
  68.1 57.4 %all-gather.2.cloned.1.call-done = bf16[2048,1,2,1024]{3,0,2,1:T(8,128)(2,1)} async-done(((bf16[512,1,2,1024]{3,0,2,1:T(8,128)(2,1)}), bf16[2048,1,2,1024]{3,0,2,1:T(8,128)(2,1)}) %all-gather.2.cloned.1.call-update) | async-done | bytes 8388624 | tf_op jit(solution)/shard_map/all_gather | solution.py:15
  125.6 16.4 %copy.8 = bf16[2048,1,2,1024]{3,2,0,1:T(2,128)(2,1)} copy(bf16[2048,1,2,1024]{3,0,2,1:T(8,128)(2,1)} %all-gather.2.cloned.1.call-done) | data formatting | bytes 16777216 | tf_op jit(solution)/shard_map/all_gather | solution.py:15
  142.0 10.1 %copy.9 = bf16[256,8,2,1024]{3,1,2,0:T(8,128)(2,1)} copy(bf16[256,8,2,1024]{3,2,1,0:T(2,128)(2,1)} %bitcast.13) | data formatting | bytes 16777216
  152.1 20.8 %gather_fusion = bf16[2048,2048]{1,0:T(8,128)(2,1)} fusion(bf16[2048,2048]{1,0:T(8,128)(2,1)} %bitcast.12, s32[2048]{0:T(1024)S(1)} %broadcast_clamp_fusion), kind=kCustom, calls=%fused_computation | custom fusion | bytes 16785408 | tf_op jit(solution)/shard_map/jit(_take)/gather | solution.py:26
  172.9 7.5 %broadcast_select_fusion = bf16[2048,2048]{1,0:T(8,128)(2,1)} fusion(bf16[2048,2048]{1,0:T(8,128)(2,1)} %gather_fusion, pred[2048]{0:T(1024)(128)(4,1)S(1)} %get-tuple-element.5), kind=kLoop, calls=%fused_computation.2 | loop fusion | flops 4194304 | bytes 16779264 | tf_op jit(solution)/shard_map/jit(_take)/select_n | solution.py:26
  180.4 0.0 copy-start
  180.4 1.9 constant_dynamic-slice_fusion
  182.3 2.2 %fusion.16 = (bf16[512,1024]{1,0:T(8,128)(2,1)S(1)}, bf16[512,1024]{1,0:T(8,128)(2,1)S(1)}) fusion(bf16[2048,2048]{1,0:T(8,128)(2,1)} %broadcast_select_fusion, s32[]{:T(128)S(6)} %select_n.36, s32[]{:T(128)S(6)} %add.37), kind=kLoop, calls=%fused_computation.38 | loop fusion | flops 1572864 | bytes 4194312 | tf_op jit(solution)/shard_map/slice | solution.py:28
  184.4 0.6 copy-done
  185.0 10.4 %multiply_convert_fusion = bf16[1024,2048]{1,0:T(8,128)(2,1)} fusion(bf16[2048,2048]{1,0:T(8,128)(2,1)S(1)} %copy-done, bf16[512,1024]{1,0:T(8,128)(2,1)S(1)} %get-tuple-element.8, bf16[512,1024]{1,0:T(8,128)(2,1)S(1)} %get-tuple-element.7, bf16[512,2048]{1,0:T(8,128)(2,1)S(1)} %constant_dynamic-slice_fusion), kind=kOutput, calls=%fused_computation.1 | convolution fusion | flops 8606711808 | bytes 16777216 | tf_op jit(solution)/shard_map/dot_general | solution.py:30
  (3 shorter events, 0.1 us)
Async XLA Ops:
  6.5 11.5 %copy-start.2 = (s32[1,1024]{1,0:T(1,128)S(1)}, s32[1,1024]{1,0:T(1,128)}, u32[]{:S(2)}) copy-start(s32[1,1024]{1,0:T(1,128)} %param.4) | copy-start | bytes 12292
  10.6 57.5 %copy-start.1 = (s32[2048]{0:T(1024)S(1)}, s32[2048]{0:T(1024)}, u32[]{:S(2)}) copy-start(s32[2048]{0:T(1024)} %param.5) | copy-start | bytes 24580
  10.6 55.7 %all-to-all-start = ((bf16[64,8,2,1024]{3,0,2,1:T(8,128)(2,1)}), bf16[64,8,2,1024]{3,0,2,1:T(8,128)(2,1)S(1)}, u32[]{:S(2)}, u32[]{:S(2)}) async-start(bf16[64,8,2,1024]{3,0,2,1:T(8,128)(2,1)} %copy.6), calls=%async_computation | async-start | bytes 4194304 | tf_op jit(solution)/shard_map/all_to_all | solution.py:13
  18.0 107.5 %all-gather.2.cloned.1.call-start = ((), (), s32[]{:S(2)}) async-start(), calls=%async_computation.1 | async-start | bytes 10485760 | tf_op jit(solution)/shard_map/all_gather | solution.py:15
  180.4 4.6 %copy-start = (bf16[2048,2048]{1,0:T(8,128)(2,1)S(1)}, bf16[2048,2048]{1,0:T(8,128)(2,1)}, u32[]{:S(2)}) copy-start(bf16[2048,2048]{1,0:T(8,128)(2,1)} %broadcast_select_fusion) | copy-start | bytes 25165828
Sparse Core Ops, SparseCore 0:
  68.2 57.3 all-gather.1
where the time goes:
time: 203 us; the launch traced here: 202 us
  waiting for transfers between devices  106 us (52%)
  local copies, waits for them, and re-layouts  54.1 us (27%)
  between operations  13.5 us (7%)
  other arithmetic  11.3 us (6%)
  matrix products  10.4 us (5%)
  starting transfers between devices  7.45 us (4%)
    all_gather x1, waiting for transfers between devices, local(): kept = lax.all_gather(turned, 'pair', axis=0, tiled=True)  57.4 us
    all_to_all x1, waiting for transfers between devices, local(): lax.all_to_all(samples, 'freq', split_axis=1, concat_axis=0, tiled=True)  48.2 us
    gather x1, local copies, waits for them, and re-layouts, local(): columns = jnp.take(feeds_all, position, axis=0)  20.8 us
    all_gather x1, local copies, waits for them, and re-layouts, local(): kept = lax.all_gather(turned, 'pair', axis=0, tiled=True)  16.4 us
    unnamed x8, local copies, waits for them, and re-layouts  14.8 us
    dot_general x1, matrix products, local(): lax.dot_general(stacked, columns, (((1,), (1,)), ((), ())), preferred_ele...  10.4 us
    select_n x1, other arithmetic, local(): columns = jnp.take(feeds_all, position, axis=0)  7.45 us
    all_to_all x1, starting transfers between devices, local(): lax.all_to_all(samples, 'freq', split_axis=1, concat_axis=0, tiled=True)  7.41 us
  transfers between devices with their start and end apart: 2, of which 2 were waited for; matrix products, arithmetic and copies ran while one was open for 0% of the time, Pallas kernels for 0%

commit v1 on v0

v1 whole, which is shorter than its diff:
```python
import functools

import jax
import jax.numpy as jnp
from jax import lax
from jax.experimental import pallas as pl
from jax.experimental.pallas import tpu as pltpu
from jax.sharding import PartitionSpec as P

LANES = 128
GROUP = 16
HALVES = 2


def tiles(samples, channel, half, halves):
    feeds, _, _, times = samples.shape
    span = times // halves
    part = lax.dynamic_slice(samples, (0, channel, 0, half * span), (feeds, 1, 2, span))[:, 0]
    blocks = span // LANES
    return part.reshape(feeds, 2, blocks, LANES).transpose(0, 2, 1, 3).reshape(feeds, 2 * blocks, LANES)


def correlate(layout, scale, last, *refs):
    if last:
        place, member, mask, total, *refs = refs
    else:
        place, member, mask, *refs = refs
    pieces, (out, held, ordered, left, sems) = refs[:-5], refs[-5:]
    step = pl.program_id(0)
    rows = left.shape[0] // 2
    deep = held.shape[1]
    block = ordered.shape[0] // pl.num_programs(0)

    @pl.when(step == 0)
    def _():
        copies = []
        for n, (piece, (source, row)) in enumerate(zip(pieces, layout)):
            src = piece if source is None else piece.at[:, pl.ds(source, deep), :]
            copies.append(pltpu.make_async_copy(src, held.at[pl.ds(row, piece.shape[0])], sems.at[n]))
        for copy in copies:
            copy.start()
        for copy in copies:
            copy.wait()

        def gather(group, carry):
            base = pl.multiple_of(group * GROUP, GROUP)
            feeds = jnp.stack([held[place[base + i]] for i in range(GROUP)], 0)
            turned = jnp.transpose(feeds, (1, 0, 2))
            for s in range(deep):
                ordered[pl.ds(base, GROUP), s * LANES : (s + 1) * LANES] = turned[s]
            return carry

        lax.fori_loop(0, ordered.shape[0] // GROUP, gather, 0)
        own = pl.ds(pl.multiple_of(member[0] * rows, GROUP), rows)
        for s in range(deep):
            here = slice(s * LANES, (s + 1) * LANES)
            there = slice((s ^ 1) * LANES, (s ^ 1) * LANES + LANES)
            left[:rows, here] = ordered[own, here] * mask[:, here]
            value = ordered[own, there] * mask[:, here]
            left[rows:, here] = value if s % 2 == 0 else -value

    columns = ordered[pl.ds(pl.multiple_of(step * block, block), block), :]
    product = lax.dot_general(
        left[...], columns, (((1,), (1,)), ((), ())), preferred_element_type=jnp.float32
    )
    if last:
        out[...] = ((product + total[...]) * scale).astype(out.dtype)
    else:
        out[...] = product


def local(samples, rfi_flags, feed_map):
    n_pair, n_freq = lax.axis_size("pair"), lax.axis_size("freq")
    me, member = lax.axis_index("freq"), lax.axis_index("pair")
    feeds, _, _, times = samples.shape
    slots = feed_map.shape[0]
    rows = slots // n_pair

    def over_freq(x, k):
        return lax.ppermute(x, "freq", [(i, i ^ k) for i in range(n_freq)])

    def over_pair(x, k):
        return lax.ppermute(x, "pair", [(i, i ^ k) for i in range(n_pair)])

    near = range(1, n_freq // 2)
    far = [range(k, min(k + 2, n_freq)) for k in range(n_freq // 2, n_freq, 2)]
    groups = []

    def spread(mine, ks, half):
        pieces = {0: mine}
        other = n_pair // 2
        if n_pair > 1:
            pieces[other] = over_pair(mine, other)
            span = 1
            while span < other:
                for m in list(pieces):
                    if m ^ span not in pieces:
                        pieces[m ^ span] = over_pair(pieces[m], span)
                span *= 2
        groups.append((list(ks), half, pieces))

    arrived = {}

    def send(k, half, halves):
        arrived[k, half] = over_freq(tiles(samples, me ^ k, half, halves), k)

    for k in far[0]:
        send(k, 0, HALVES)
    for k in near:
        send(k, 0, 1)
    for half in range(HALVES):
        for ks in far:
            for k in ks:
                if (k, half) not in arrived or (k in near):
                    send(k, half, HALVES)
    own = tiles(samples, me, 0, 1)
    spread(own, [0], None)
    if len(near):
        spread(jnp.concatenate([arrived[k, 0] for k in near]), near, None)
    for half in range(HALVES):
        for ks in far:
            spread(jnp.concatenate([arrived[k, half] for k in ks]), ks, half)

    device, within = feed_map // feeds, feed_map % feeds
    hop, other = (device // n_pair) ^ me, (device % n_pair) ^ member
    keep = (1 - rfi_flags).astype(jnp.bfloat16).reshape(times // LANES, 1, LANES)
    keep = jnp.broadcast_to(keep, (times // LANES, 2, LANES)).reshape(1, 2 * times)
    deep = 2 * times // LANES // HALVES
    total = None
    for half in range(HALVES):
        arrays, layout, row = [], [], 0
        start = {}
        for ks, which, pieces in groups:
            if which is not None and which != half:
                continue
            for m, array in pieces.items():
                arrays.append(array)
                layout.append((None if which is not None else half * deep, row))
                for n, k in enumerate(ks):
                    start[k, m] = row + n * feeds
                row += array.shape[0]
        table = jnp.array([start[k, m] for k in range(n_freq) for m in range(n_pair)], jnp.int32)
        place = table[hop * n_pair + other] + within
        last = half == HALVES - 1
        steps = 8
        width = slots // steps
        mask = keep[:, half * deep * LANES : (half + 1) * deep * LANES]
        smem = pl.BlockSpec(memory_space=pltpu.SMEM)
        block = pl.BlockSpec((2 * rows, width), lambda i: (0, i))
        in_specs = [smem, smem, pl.BlockSpec(mask.shape, lambda i: (0, 0))]
        operands = [place, member.reshape(1), mask]
        if last:
            in_specs.append(block)
            operands.append(total)
        in_specs += [pl.BlockSpec(memory_space=pl.ANY)] * len(arrays)
        total = pl.pallas_call(
            functools.partial(correlate, layout, 1.0 / times, last),
            out_shape=jax.ShapeDtypeStruct((2 * rows, slots), jnp.bfloat16 if last else jnp.float32),
            grid=(steps,),
            in_specs=in_specs,
            out_specs=block,
            scratch_shapes=[
                pltpu.VMEM((slots, deep, LANES), jnp.bfloat16),
                pltpu.VMEM((slots, deep * LANES), jnp.bfloat16),
                pltpu.VMEM((2 * rows, deep * LANES), jnp.bfloat16),
                pltpu.SemaphoreType.DMA((len(arrays),)),
            ],
            compiler_params=pltpu.CompilerParams(vmem_limit_bytes=32 << 20),
        )(*operands, *arrays)
    return total.reshape(1, 2, rows, slots)


def solution(mesh):
    in_specs = (P(("freq", "pair"), None, None, None), P("freq", None), P())
    out_specs = P("freq", None, "pair", None)
    return jax.shard_map(local, mesh=mesh, in_specs=in_specs, out_specs=out_specs, check_vma=False)
```

time: 203 us -> 132 us (0.65)
  waiting for transfers between devices: 106 us -> 62.1 us
  local copies, waits for them, and re-layouts: 54.1 us -> 11.7 us
  Pallas kernels: 0 us -> 27.3 us
  starting transfers between devices: 7.45 us -> 30.3 us
  between operations: 13.5 us -> 0.35 us
  other arithmetic: 11.3 us -> 0.07 us
  matrix products: 10.4 us -> 0 us
    ppermute x0 -> x29, waiting for transfers between devices: none -> 62.1 us  [the longest x18 33 us: over_pair(): return lax.ppermute(x, 'pair', [(i, i ^ k) for i in range(n_pair)])]
    all_gather x1 -> x0, waiting for transfers between devices: 57.4 us -> none  [local(): kept = lax.all_gather(turned, 'pair', axis=0, tiled=True)]
    all_to_all x1 -> x0, waiting for transfers between devices: 48.2 us -> none  [local(): lax.all_to_all(samples, 'freq', split_axis=1, concat_axis=0, tiled=True)]
    ppermute x0 -> x29, starting transfers between devices: none -> 30.3 us  [the longest x11 22.5 us: over_freq(): return lax.ppermute(x, 'freq', [(i, i ^ k) for i in range(n_freq)])]
    pallas_call x0 -> x2, Pallas kernels: none -> 27.3 us  [local(): pl.pallas_call(functools.partial(correlate, layout, 1.0 / times, last), o...]
    gather x1 -> x0, local copies, waits for them, and re-layouts: 20.8 us -> none  [local(): columns = jnp.take(feeds_all, position, axis=0)]
    all_gather x1 -> x0, local copies, waits for them, and re-layouts: 16.4 us -> none  [local(): kept = lax.all_gather(turned, 'pair', axis=0, tiled=True)]
    dot_general x1 -> x0, matrix products: 10.4 us -> none  [local(): lax.dot_general(stacked, columns, (((1,), (1,)), ((), ())), preferred_ele...]
  transfers between devices with their start and end apart: 2 -> 29, of which waited for: 2 -> 10; matrix products, arithmetic and copies ran while one was open for 0% -> 1% of each run, Pallas kernels for 0% -> 10%
where the time goes in v1:
time: 132 us
  waiting for transfers between devices  62.1 us (47%)
  starting transfers between devices  30.3 us (23%)
  Pallas kernels  27.3 us (21%)
  local copies, waits for them, and re-layouts  11.7 us (9%)
    ppermute x18, waiting for transfers between devices, over_pair(): return lax.ppermute(x, 'pair', [(i, i ^ k) for i in range(n_pair)])  33 us
    ppermute x11, waiting for transfers between devices, over_freq(): return lax.ppermute(x, 'freq', [(i, i ^ k) for i in range(n_freq)])  29 us
    pallas_call x2, Pallas kernels, local(): pl.pallas_call(functools.partial(correlate, layout, 1.0 / times, last), o...  27.3 us
    ppermute x11, starting transfers between devices, over_freq(): return lax.ppermute(x, 'freq', [(i, i ^ k) for i in range(n_freq)])  22.5 us
    unnamed x50, local copies, waits for them, and re-layouts  8.4 us
    ppermute x18, starting transfers between devices, over_pair(): return lax.ppermute(x, 'pair', [(i, i ^ k) for i in range(n_pair)])  7.83 us
    dynamic_slice x2, local copies, waits for them, and re-layouts, tiles(): lax.dynamic_slice(samples, (0, channel, 0, half * span), (feeds, 1, 2, sp...  3.19 us
  transfers between devices with their start and end apart: 29, of which 10 were waited for; matrix products, arithmetic and copies ran while one was open for 1% of the time, Pallas kernels for 10%

profile of v1, /device:TPU:0, one launch (start us, length us, event | category | flops | bytes accessed | tf_op | source)
XLA Modules:
  0.0 131.9 jit_solution(16363044427323294317)
XLA Ops:
  0.0 2.2 %constant_dynamic-slice_fusion = (bf16[64,1,2,512]{3,2,1,0:T(2,128)(2,1)S(1)}, bf16[64,1,2,512]{3,2,1,0:T(2,128)(2,1)S(1)}, bf16[64,1,2,512]{3,2,1,0:T(2,128)(2,...) fusion(bf16[64,8,2,1024]{3,2,1,0:T(2,128)(2,1)} %param.5, ...), kind=kLoop, calls=%fused_computation.36 | loop fusion | bytes 2097168 | tf_op jit(solution)/shard_map/dynamic_slice | solution.py:18
  2.2 4.1 %collective-permute-start.19 = (bf16[64,8,128]{2,1,0:T(8,128)(2,1)S(1)}, bf16[64,8,128]{2,1,0:T(8,128)(2,1)S(1)}, u32[]{:S(2)}, u32[]{:S(2)}) collective-permute-start(bf16[64,8,128]{2,1,0:T(8,128)(2,1)S(1)} %bitcast.77), channel_id=1, source_target_pairs={{0,16},{4,20},{8,24},{12,28},{16,0},{20,4},{24,8},{28,12},{1,17},{... | collective-permute-start | bytes 393224 | tf_op jit(solution)/shard_map/ppermute | solution.py:80
  6.3 1.0 constant_dynamic-slice_fusion.8
  7.3 0.0 copy-start.20
  7.4 1.6 %collective-permute-start.3 = (bf16[64,16,128]{2,1,0:T(8,128)(2,1)S(1)}, bf16[64,16,128]{2,1,0:T(8,128)(2,1)S(1)}, u32[]{:S(2)}, u32[]{:S(2)}) collective-permute-start(bf16[64,16,128]{2,1,0:T(8,128)(2,1)S(1)} %bitcast.69), channel_id=1, source_target_pairs={{0,4},{4,0},{8,12},{12,8},{16,20},{20,16},{24,28},{28,24},{1,5},{5... | collective-permute-start | bytes 786440 | tf_op jit(solution)/shard_map/ppermute | solution.py:80
  8.9 0.3 collective-permute-start.9
  9.2 2.6 %collective-permute-start.20 = (bf16[64,8,128]{2,1,0:T(8,128)(2,1)S(1)}, bf16[64,8,128]{2,1,0:T(8,128)(2,1)S(1)}, u32[]{:S(2)}, u32[]{:S(2)}) collective-permute-start(bf16[64,8,128]{2,1,0:T(8,128)(2,1)S(1)} %bitcast.75), channel_id=1, source_target_pairs={{0,20},{4,16},{8,28},{12,24},{16,4},{20,0},{24,12},{28,8},{1,21},{... | collective-permute-start | bytes 393224 | tf_op jit(solution)/shard_map/ppermute | solution.py:80
  11.8 2.3 %collective-permute-start.25 = (bf16[64,8,128]{2,1,0:T(8,128)(2,1)S(1)}, bf16[64,8,128]{2,1,0:T(8,128)(2,1)S(1)}, u32[]{:S(2)}, u32[]{:S(2)}) collective-permute-start(bf16[64,8,128]{2,1,0:T(8,128)(2,1)S(1)} %bitcast.73), channel_id=1, source_target_pairs={{0,28},{4,24},{8,20},{12,16},{16,12},{20,8},{24,4},{28,0},{1,29},{... | collective-permute-start | bytes 393224 | tf_op jit(solution)/shard_map/ppermute | solution.py:80
  14.1 7.8 %collective-permute-done.19 = bf16[64,8,128]{2,1,0:T(8,128)(2,1)S(1)} collective-permute-done((bf16[64,8,128]{2,1,0:T(8,128)(2,1)S(1)}, bf16[64,8,128]{2,1,0:T(8,128)(2,1)S(1)}, u32[]{:S(2)}, u32[]{:S(2)}) %collective-permute-start.19) | collective-permute-done | bytes 131104 | tf_op jit(solution)/shard_map/ppermute | solution.py:80
  21.9 2.9 %collective-permute-done.9 = bf16[64,8,128]{2,1,0:T(8,128)(2,1)S(1)} collective-permute-done((bf16[64,8,128]{2,1,0:T(8,128)(2,1)S(1)}, bf16[64,8,128]{2,1,0:T(8,128)(2,1)S(1)}, u32[]{:S(2)}, u32[]{:S(2)}) %collective-permute-start.9) | collective-permute-done | bytes 131104 | tf_op jit(solution)/shard_map/ppermute | solution.py:80
  24.8 0.8 collective-permute-start.5
  25.6 3.4 %collective-permute-start.10 = (bf16[64,8,128]{2,1,0:T(8,128)(2,1)S(1)}, bf16[64,8,128]{2,1,0:T(8,128)(2,1)S(1)}, u32[]{:S(2)}, u32[]{:S(2)}) collective-permute-start(bf16[64,8,128]{2,1,0:T(8,128)(2,1)S(1)} %bitcast.72), channel_id=1, source_target_pairs={{0,20},{4,16},{8,28},{12,24},{16,4},{20,0},{24,12},{28,8},{1,21},{... | collective-permute-start | bytes 393224 | tf_op jit(solution)/shard_map/ppermute | solution.py:80
  29.1 6.1 %collective-permute-done.4 = bf16[64,16,128]{2,1,0:T(8,128)(2,1)S(1)} collective-permute-done((bf16[64,16,128]{2,1,0:T(8,128)(2,1)S(1)}, bf16[64,16,128]{2,1,0:T(8,128)(2,1)S(1)}, u32[]{:S(2)}, u32[]{:S(2)}) %collective-permute-start.4) | collective-permute-done | bytes 262176 | tf_op jit(solution)/shard_map/ppermute | solution.py:80
  35.2 3.5 %collective-permute-start.24 = (bf16[64,8,128]{2,1,0:T(8,128)(2,1)S(1)}, bf16[64,8,128]{2,1,0:T(8,128)(2,1)S(1)}, u32[]{:S(2)}, u32[]{:S(2)}) collective-permute-start(bf16[64,8,128]{2,1,0:T(8,128)(2,1)S(1)} %bitcast.74), channel_id=1, source_target_pairs={{0,24},{4,28},{8,16},{12,20},{16,8},{20,12},{24,0},{28,4},{1,25},{... | collective-permute-start | bytes 393224 | tf_op jit(solution)/shard_map/ppermute | solution.py:80
  38.8 5.7 %collective-permute-done.5 = bf16[64,16,128]{2,1,0:T(8,128)(2,1)S(1)} collective-permute-done((bf16[64,16,128]{2,1,0:T(8,128)(2,1)S(1)}, bf16[64,16,128]{2,1,0:T(8,128)(2,1)S(1)}, u32[]{:S(2)}, u32[]{:S(2)}) %collective-permute-start.5) | collective-permute-done | bytes 262176 | tf_op jit(solution)/shard_map/ppermute | solution.py:80
  44.5 0.0 collective-permute-start.1
  44.6 1.6 %collective-permute-start = (bf16[64,16,128]{2,1,0:T(8,128)(2,1)S(1)}, bf16[64,16,128]{2,1,0:T(8,128)(2,1)}, u32[]{:S(2)}, u32[]{:S(2)}) collective-permute-start(bf16[64,16,128]{2,1,0:T(8,128)(2,1)S(1)} %bitcast.64), channel_id=1, source_target_pairs={{0,2},{1,3},{2,0},{3,1},{4,6},{5,7},{6,4},{7,5},{8,10},{9,11},{10,... | collective-permute-start | bytes 786440 | tf_op jit(solution)/shard_map/ppermute | solution.py:83
  46.1 0.5 collective-permute-start.6
  46.7 3.5 %collective-permute-start.15 = (bf16[64,8,128]{2,1,0:T(8,128)(2,1)S(1)}, bf16[64,8,128]{2,1,0:T(8,128)(2,1)S(1)}, u32[]{:S(2)}, u32[]{:S(2)}) collective-permute-start(bf16[64,8,128]{2,1,0:T(8,128)(2,1)S(1)} %bitcast.71), channel_id=1, source_target_pairs={{0,28},{4,24},{8,20},{12,16},{16,12},{20,8},{24,4},{28,0},{1,29},{... | collective-permute-start | bytes 393224 | tf_op jit(solution)/shard_map/ppermute | solution.py:80
  50.2 0.3 collective-permute-start.14
  50.6 4.3 %collective-permute-done.15 = bf16[64,8,128]{2,1,0:T(8,128)(2,1)S(1)} collective-permute-done((bf16[64,8,128]{2,1,0:T(8,128)(2,1)S(1)}, bf16[64,8,128]{2,1,0:T(8,128)(2,1)S(1)}, u32[]{:S(2)}, u32[]{:S(2)}) %collective-permute-start.15) | collective-permute-done | bytes 131104 | tf_op jit(solution)/shard_map/ppermute | solution.py:80
  54.9 2.2 %collective-permute-done.14 = bf16[64,8,128]{2,1,0:T(8,128)(2,1)S(1)} collective-permute-done((bf16[64,8,128]{2,1,0:T(8,128)(2,1)S(1)}, bf16[64,8,128]{2,1,0:T(8,128)(2,1)S(1)}, u32[]{:S(2)}, u32[]{:S(2)}) %collective-permute-start.14) | collective-permute-done | bytes 131104 | tf_op jit(solution)/shard_map/ppermute | solution.py:80
  57.1 1.5 %collective-permute-start.11 = (bf16[128,8,128]{2,1,0:T(8,128)(2,1)S(1)}, bf16[128,8,128]{2,1,0:T(8,128)(2,1)}, u32[]{:S(2)}, u32[]{:S(2)}) collective-permute-start(bf16[128,8,128]{2,1,0:T(8,128)(2,1)S(1)} %constant_dynamic-update-slice_fusion.3.refs_11_), channel_id=1, source_target_pairs={{0,2},{1,3},{2,0},{3,1},{4,6},{5,7},{6,4},{7,5},{8,10},{9,11},{10,... | collective-permute-start | bytes 786440 | tf_op jit(solution)/shard_map/ppermute | solution.py:83
  58.6 0.7 copy-done
  59.3 0.5 collective-permute-start.26
  59.9 21.5 %collective-permute-done.26.refs_17_ = bf16[128,8,128]{2,1,0:T(8,128)(2,1)S(1)} collective-permute-done((bf16[128,8,128]{2,1,0:T(8,128)(2,1)S(1)}, bf16[128,8,128]{2,1,0:T(8,128)(2,1)S(1)}, u32[]{:S(2)}, u32[]{:S(2)}) %collective-permute-start.26) | collective-permute-done | bytes 262176 | tf_op jit(solution)/shard_map/ppermute | solution.py:83
  81.4 0.7 copy-done.13
  82.2 1.5 %collective-permute-start.16 = (bf16[128,8,128]{2,1,0:T(8,128)(2,1)S(1)}, bf16[128,8,128]{2,1,0:T(8,128)(2,1)}, u32[]{:S(2)}, u32[]{:S(2)}) collective-permute-start(bf16[128,8,128]{2,1,0:T(8,128)(2,1)S(1)} %constant_dynamic-update-slice_fusion.5.refs_15_), channel_id=1, source_target_pairs={{0,2},{1,3},{2,0},{3,1},{4,6},{5,7},{6,4},{7,5},{8,10},{9,11},{10,... | collective-permute-start | bytes 786440 | tf_op jit(solution)/shard_map/ppermute | solution.py:83
  83.7 0.7 copy-done.9
  84.4 0.5 collective-permute-start.21
  84.9 0.7 copy-done.17
  85.6 0.5 collective-permute-start.2
  86.1 5.3 %collective-permute-done.16.refs_16_ = bf16[128,8,128]{2,1,0:T(8,128)(2,1)} collective-permute-done((bf16[128,8,128]{2,1,0:T(8,128)(2,1)S(1)}, bf16[128,8,128]{2,1,0:T(8,128)(2,1)}, u32[]{:S(2)}, u32[]{:S(2)}) %collective-permute-start.16) | collective-permute-done | bytes 262176 | tf_op jit(solution)/shard_map/ppermute | solution.py:83
  91.4 5.0 %collective-permute-done.21.refs_13_ = bf16[128,8,128]{2,1,0:T(8,128)(2,1)S(1)} collective-permute-done((bf16[128,8,128]{2,1,0:T(8,128)(2,1)S(1)}, bf16[128,8,128]{2,1,0:T(8,128)(2,1)S(1)}, u32[]{:S(2)}, u32[]{:S(2)}) %collective-permute-start.21) | collective-permute-done | bytes 262176 | tf_op jit(solution)/shard_map/ppermute | solution.py:83
  96.5 0.7 copy-done.15
  97.2 0.6 collective-permute-start.27
  97.8 0.1 collective-permute-start.22
  97.9 1.1 collective-permute-done.18.refs_18_
  99.0 0.1 collective-permute-start.28
  99.2 0.4 collective-permute-start.23
  99.6 0.0 copy-start.1
  99.7 0.9 copy-done.1
  100.6 0.9 copy-done.6
  101.5 0.9 copy-done.10
  102.5 0.9 copy-done.14
  103.4 0.9 copy-done.18
  104.4 13.2 %shard_map.55.refs_3_ = f32[1024,2048]{1,0:T(8,128)S(1)} custom-call(s32[2048]{0:T(1024)S(1)} %fusion.4.refs_0_, s32[1]{0:T(128)} %bitcast.refs_1_, bf16[1,1024]{1,0:T(2,128)(2,1)S(1)} %get-tuple-element.17.refs_2_, bf16[64,16,128]{2,1,0:T(8,128)(2,1)S(1)} %bitcast.65, bf16[64,16,128]{2,1,0:T(8,128)(2,1)} %collective-permute-done.refs_4_.refs_5_, ...), custom_call_target="tpu_custom_call" | custom-call | tf_op jit(solution)/shard_map/pallas_call | solution.py:156
  117.7 14.2 %shard_map.56 = bf16[1024,2048]{1,0:T(8,128)(2,1)} custom-call(s32[2048]{0:T(1024)S(1)} %fusion.4.refs_0_, s32[1]{0:T(128)} %bitcast.refs_1_, bf16[1,1024]{1,0:T(2,128)(2,1)S(1)} %get-tuple-element.18.refs_2_, f32[1024,2048]{1,0:T(8,128)S(1)} %shard_map.55.refs_3_, bf16[64,16,128]{2,1,0:T(8,128)(2,1)S(1)} %bitcast.66, ...), custom_call_target="tpu_custom_call" | custom-call | tf_op jit(solution)/shard_map/pallas_call | solution.py:156
  (74 shorter events, 0.4 us)
Async XLA Ops:
  0.0 6.3 %copy-start.19 = (bf16[64,8,2,1024]{3,2,1,0:T(2,128)(2,1)S(1)}, bf16[64,8,2,1024]{3,2,1,0:T(2,128)(2,1)}, u32[]{:S(2)}) copy-start(bf16[64,8,2,1024]{3,2,1,0:T(2,128)(2,1)} %param.5) | copy-start | bytes 6291460
  2.2 19.7 %collective-permute-start.19 = (bf16[64,8,128]{2,1,0:T(8,128)(2,1)S(1)}, bf16[64,8,128]{2,1,0:T(8,128)(2,1)S(1)}, u32[]{:S(2)}, u32[]{:S(2)}) collective-permute-start(bf16[64,8,128]{2,1,0:T(8,128)(2,1)S(1)} %bitcast.77), channel_id=1, source_target_pairs={{0,16},{4,20},{8,24},{12,28},{16,0},{20,4},{24,8},{28,12},{1,17},{... | collective-permute-start | bytes 393224 | tf_op jit(solution)/shard_map/ppermute | solution.py:80
  7.3 89.8 %copy-start.21 = (s32[1,1024]{1,0:T(1,128)S(1)}, s32[1,1024]{1,0:T(1,128)}, u32[]{:S(2)}) copy-start(s32[1,1024]{1,0:T(1,128)} %param.6) | copy-start | bytes 12292
  7.3 92.2 %copy-start.20 = (s32[2048]{0:T(1024)S(1)}, s32[2048]{0:T(1024)}, u32[]{:S(2)}) copy-start(s32[2048]{0:T(1024)} %param.7) | copy-start | bytes 24580
  7.4 18.3 %collective-permute-start.3 = (bf16[64,16,128]{2,1,0:T(8,128)(2,1)S(1)}, bf16[64,16,128]{2,1,0:T(8,128)(2,1)S(1)}, u32[]{:S(2)}, u32[]{:S(2)}) collective-permute-start(bf16[64,16,128]{2,1,0:T(8,128)(2,1)S(1)} %bitcast.69), channel_id=1, source_target_pairs={{0,4},{4,0},{8,12},{12,8},{16,20},{20,16},{24,28},{28,24},{1,5},{5... | collective-permute-start | bytes 786440 | tf_op jit(solution)/shard_map/ppermute | solution.py:80
  8.9 15.9 %collective-permute-start.9 = (bf16[64,8,128]{2,1,0:T(8,128)(2,1)S(1)}, bf16[64,8,128]{2,1,0:T(8,128)(2,1)S(1)}, u32[]{:S(2)}, u32[]{:S(2)}) collective-permute-start(bf16[64,8,128]{2,1,0:T(8,128)(2,1)S(1)} %bitcast.76), channel_id=1, source_target_pairs={{0,16},{4,20},{8,24},{12,28},{16,0},{20,4},{24,8},{28,12},{1,17},{... | collective-permute-start | bytes 393224 | tf_op jit(solution)/shard_map/ppermute | solution.py:80
  9.2 35.3 %collective-permute-start.20 = (bf16[64,8,128]{2,1,0:T(8,128)(2,1)S(1)}, bf16[64,8,128]{2,1,0:T(8,128)(2,1)S(1)}, u32[]{:S(2)}, u32[]{:S(2)}) collective-permute-start(bf16[64,8,128]{2,1,0:T(8,128)(2,1)S(1)} %bitcast.75), channel_id=1, source_target_pairs={{0,20},{4,16},{8,28},{12,24},{16,4},{20,0},{24,12},{28,8},{1,21},{... | collective-permute-start | bytes 393224 | tf_op jit(solution)/shard_map/ppermute | solution.py:80
  11.8 34.9 %collective-permute-start.25 = (bf16[64,8,128]{2,1,0:T(8,128)(2,1)S(1)}, bf16[64,8,128]{2,1,0:T(8,128)(2,1)S(1)}, u32[]{:S(2)}, u32[]{:S(2)}) collective-permute-start(bf16[64,8,128]{2,1,0:T(8,128)(2,1)S(1)} %bitcast.73), channel_id=1, source_target_pairs={{0,28},{4,24},{8,20},{12,16},{16,12},{20,8},{24,4},{28,0},{1,29},{... | collective-permute-start | bytes 393224 | tf_op jit(solution)/shard_map/ppermute | solution.py:80
  21.9 13.3 %collective-permute-start.4 = (bf16[64,16,128]{2,1,0:T(8,128)(2,1)S(1)}, bf16[64,16,128]{2,1,0:T(8,128)(2,1)S(1)}, u32[]{:S(2)}, u32[]{:S(2)}) collective-permute-start(bf16[64,16,128]{2,1,0:T(8,128)(2,1)S(1)} %bitcast.68), channel_id=1, source_target_pairs={{0,8},{4,12},{8,0},{12,4},{16,24},{20,28},{24,16},{28,20},{1,9},{5... | collective-permute-start | bytes 786440 | tf_op jit(solution)/shard_map/ppermute | solution.py:80
  24.8 19.7 %collective-permute-start.5 = (bf16[64,16,128]{2,1,0:T(8,128)(2,1)S(1)}, bf16[64,16,128]{2,1,0:T(8,128)(2,1)S(1)}, u32[]{:S(2)}, u32[]{:S(2)}) collective-permute-start(bf16[64,16,128]{2,1,0:T(8,128)(2,1)S(1)} %bitcast.67), channel_id=1, source_target_pairs={{0,12},{4,8},{8,4},{12,0},{16,28},{20,24},{24,20},{28,16},{1,13},{... | collective-permute-start | bytes 786440 | tf_op jit(solution)/shard_map/ppermute | solution.py:80
  25.6 24.6 %collective-permute-start.10 = (bf16[64,8,128]{2,1,0:T(8,128)(2,1)S(1)}, bf16[64,8,128]{2,1,0:T(8,128)(2,1)S(1)}, u32[]{:S(2)}, u32[]{:S(2)}) collective-permute-start(bf16[64,8,128]{2,1,0:T(8,128)(2,1)S(1)} %bitcast.72), channel_id=1, source_target_pairs={{0,20},{4,16},{8,28},{12,24},{16,4},{20,0},{24,12},{28,8},{1,21},{... | collective-permute-start | bytes 393224 | tf_op jit(solution)/shard_map/ppermute | solution.py:80
  35.2 11.0 %collective-permute-start.24 = (bf16[64,8,128]{2,1,0:T(8,128)(2,1)S(1)}, bf16[64,8,128]{2,1,0:T(8,128)(2,1)S(1)}, u32[]{:S(2)}, u32[]{:S(2)}) collective-permute-start(bf16[64,8,128]{2,1,0:T(8,128)(2,1)S(1)} %bitcast.74), channel_id=1, source_target_pairs={{0,24},{4,28},{8,16},{12,20},{16,8},{20,12},{24,0},{28,4},{1,25},{... | collective-permute-start | bytes 393224 | tf_op jit(solution)/shard_map/ppermute | solution.py:80
  44.5 14.1 %collective-permute-start.1 = (bf16[64,16,128]{2,1,0:T(8,128)(2,1)S(1)}, bf16[64,16,128]{2,1,0:T(8,128)(2,1)S(1)}, u32[]{:S(2)}, u32[]{:S(2)}) collective-permute-start(bf16[64,16,128]{2,1,0:T(8,128)(2,1)S(1)} %bitcast.63), channel_id=1, source_target_pairs={{0,1},{1,0},{2,3},{3,2},{4,5},{5,4},{6,7},{7,6},{8,9},{9,8},{10,11... | collective-permute-start | bytes 786440 | tf_op jit(solution)/shard_map/ppermute | solution.py:83
  44.6 15.2 %collective-permute-start = (bf16[64,16,128]{2,1,0:T(8,128)(2,1)S(1)}, bf16[64,16,128]{2,1,0:T(8,128)(2,1)}, u32[]{:S(2)}, u32[]{:S(2)}) collective-permute-start(bf16[64,16,128]{2,1,0:T(8,128)(2,1)S(1)} %bitcast.64), channel_id=1, source_target_pairs={{0,2},{1,3},{2,0},{3,1},{4,6},{5,7},{6,4},{7,5},{8,10},{9,11},{10,... | collective-permute-start | bytes 786440 | tf_op jit(solution)/shard_map/ppermute | solution.py:83
  46.1 38.7 %collective-permute-start.6 = (bf16[192,16,128]{2,1,0:T(8,128)(2,1)S(1)}, bf16[192,16,128]{2,1,0:T(8,128)(2,1)S(1)}, u32[]{:S(2)}, u32[]{:S(2)}) collective-permute-start(bf16[192,16,128]{2,1,0:T(8,128)(2,1)S(1)} %constant_dynamic-update-slice_fusion.refs_7_.refs_8_), channel_id=1, source_target_pairs={{0,2},{1,3},{2,0},{3,1},{4,6},{5,7},{6,4},{7,5},{8,10},{9,11},{10,... | collective-permute-start | bytes 2359304 | tf_op jit(solution)/shard_map/ppermute | solution.py:83
  46.7 8.2 %collective-permute-start.15 = (bf16[64,8,128]{2,1,0:T(8,128)(2,1)S(1)}, bf16[64,8,128]{2,1,0:T(8,128)(2,1)S(1)}, u32[]{:S(2)}, u32[]{:S(2)}) collective-permute-start(bf16[64,8,128]{2,1,0:T(8,128)(2,1)S(1)} %bitcast.71), channel_id=1, source_target_pairs={{0,28},{4,24},{8,20},{12,16},{16,12},{20,8},{24,4},{28,0},{1,29},{... | collective-permute-start | bytes 393224 | tf_op jit(solution)/shard_map/ppermute | solution.py:80
  50.2 6.9 %collective-permute-start.14 = (bf16[64,8,128]{2,1,0:T(8,128)(2,1)S(1)}, bf16[64,8,128]{2,1,0:T(8,128)(2,1)S(1)}, u32[]{:S(2)}, u32[]{:S(2)}) collective-permute-start(bf16[64,8,128]{2,1,0:T(8,128)(2,1)S(1)} %bitcast.70), channel_id=1, source_target_pairs={{0,24},{4,28},{8,16},{12,20},{16,8},{20,12},{24,0},{28,4},{1,25},{... | collective-permute-start | bytes 393224 | tf_op jit(solution)/shard_map/ppermute | solution.py:80
  50.5 45.9 %copy-start.5 = (bf16[128,8,128]{2,1,0:T(8,128)(2,1)}, bf16[128,8,128]{2,1,0:T(8,128)(2,1)S(1)}, u32[]{:S(2)}) copy-start(bf16[128,8,128]{2,1,0:T(8,128)(2,1)S(1)} %constant_dynamic-update-slice_fusion.3.refs_11_) | copy-start | bytes 786436
  50.5 46.6 %copy-start.7 = (bf16[128,8,128]{2,1,0:T(8,128)(2,1)}, bf16[128,8,128]{2,1,0:T(8,128)(2,1)S(1)}, u32[]{:S(2)}) copy-start(bf16[128,8,128]{2,1,0:T(8,128)(2,1)S(1)} %constant_dynamic-update-slice_fusion.9.refs_16_) | copy-start | bytes 786436
  54.9 26.5 %collective-permute-start.12 = (bf16[128,8,128]{2,1,0:T(8,128)(2,1)S(1)}, bf16[128,8,128]{2,1,0:T(8,128)(2,1)S(1)}, u32[]{:S(2)}, u32[]{:S(2)}) collective-permute-start(bf16[128,8,128]{2,1,0:T(8,128)(2,1)S(1)} %constant_dynamic-update-slice_fusion.3.refs_11_), channel_id=1, source_target_pairs={{0,1},{1,0},{2,3},{3,2},{4,5},{5,4},{6,7},{7,6},{8,9},{9,8},{10,11... | collective-permute-start | bytes 786440 | tf_op jit(solution)/shard_map/ppermute | solution.py:83
  57.1 27.3 %collective-permute-start.11 = (bf16[128,8,128]{2,1,0:T(8,128)(2,1)S(1)}, bf16[128,8,128]{2,1,0:T(8,128)(2,1)}, u32[]{:S(2)}, u32[]{:S(2)}) collective-permute-start(bf16[128,8,128]{2,1,0:T(8,128)(2,1)S(1)} %constant_dynamic-update-slice_fusion.3.refs_11_), channel_id=1, source_target_pairs={{0,2},{1,3},{2,0},{3,1},{4,6},{5,7},{6,4},{7,5},{8,10},{9,11},{10,... | collective-permute-start | bytes 786440 | tf_op jit(solution)/shard_map/ppermute | solution.py:83
  59.3 22.1 %collective-permute-start.26 = (bf16[128,8,128]{2,1,0:T(8,128)(2,1)S(1)}, bf16[128,8,128]{2,1,0:T(8,128)(2,1)S(1)}, u32[]{:S(2)}, u32[]{:S(2)}) collective-permute-start(bf16[128,8,128]{2,1,0:T(8,128)(2,1)S(1)} %constant_dynamic-update-slice_fusion.9.refs_16_), channel_id=1, source_target_pairs={{0,2},{1,3},{2,0},{3,1},{4,6},{5,7},{6,4},{7,5},{8,10},{9,11},{10,... | collective-permute-start | bytes 786440 | tf_op jit(solution)/shard_map/ppermute | solution.py:83
  59.8 39.4 %collective-permute-start.7 = (bf16[192,16,128]{2,1,0:T(8,128)(2,1)S(1)}, bf16[192,16,128]{2,1,0:T(8,128)(2,1)S(1)}, u32[]{:S(2)}, u32[]{:S(2)}) collective-permute-start(bf16[192,16,128]{2,1,0:T(8,128)(2,1)S(1)} %constant_dynamic-update-slice_fusion.refs_7_.refs_8_), channel_id=1, source_target_pairs={{0,1},{1,0},{2,3},{3,2},{4,5},{5,4},{6,7},{7,6},{8,9},{9,8},{10,11... | collective-permute-start | bytes 2359304 | tf_op jit(solution)/shard_map/ppermute | solution.py:83
  59.8 25.0 %copy-start.3 = (bf16[128,8,128]{2,1,0:T(8,128)(2,1)}, bf16[128,8,128]{2,1,0:T(8,128)(2,1)S(1)}, u32[]{:S(2)}) copy-start(bf16[128,8,128]{2,1,0:T(8,128)(2,1)S(1)} %constant_dynamic-update-slice_fusion.7.refs_12_) | copy-start | bytes 786436
  81.4 15.8 %copy-start.11 = (bf16[128,8,128]{2,1,0:T(8,128)(2,1)}, bf16[128,8,128]{2,1,0:T(8,128)(2,1)S(1)}, u32[]{:S(2)}) copy-start(bf16[128,8,128]{2,1,0:T(8,128)(2,1)S(1)} %collective-permute-done.26.refs_17_) | copy-start | bytes 786436
  81.4 3.5 %collective-permute-start.17 = (bf16[128,8,128]{2,1,0:T(8,128)(2,1)S(1)}, bf16[128,8,128]{2,1,0:T(8,128)(2,1)S(1)}, u32[]{:S(2)}, u32[]{:S(2)}) collective-permute-start(bf16[128,8,128]{2,1,0:T(8,128)(2,1)S(1)} %constant_dynamic-update-slice_fusion.5.refs_15_), channel_id=1, source_target_pairs={{0,1},{1,0},{2,3},{3,2},{4,5},{5,4},{6,7},{7,6},{8,9},{9,8},{10,11... | collective-permute-start | bytes 786440 | tf_op jit(solution)/shard_map/ppermute | solution.py:83
  81.4 0.7 copy-start.13
  82.2 9.3 %collective-permute-start.16 = (bf16[128,8,128]{2,1,0:T(8,128)(2,1)S(1)}, bf16[128,8,128]{2,1,0:T(8,128)(2,1)}, u32[]{:S(2)}, u32[]{:S(2)}) collective-permute-start(bf16[128,8,128]{2,1,0:T(8,128)(2,1)S(1)} %constant_dynamic-update-slice_fusion.5.refs_15_), channel_id=1, source_target_pairs={{0,2},{1,3},{2,0},{3,1},{4,6},{5,7},{6,4},{7,5},{8,10},{9,11},{10,... | collective-permute-start | bytes 786440 | tf_op jit(solution)/shard_map/ppermute | solution.py:83
  84.4 12.1 %collective-permute-start.21 = (bf16[128,8,128]{2,1,0:T(8,128)(2,1)S(1)}, bf16[128,8,128]{2,1,0:T(8,128)(2,1)S(1)}, u32[]{:S(2)}, u32[]{:S(2)}) collective-permute-start(bf16[128,8,128]{2,1,0:T(8,128)(2,1)S(1)} %constant_dynamic-update-slice_fusion.7.refs_12_), channel_id=1, source_target_pairs={{0,2},{1,3},{2,0},{3,1},{4,6},{5,7},{6,4},{7,5},{8,10},{9,11},{10,... | collective-permute-start | bytes 786440 | tf_op jit(solution)/shard_map/ppermute | solution.py:83
  84.9 14.7 %collective-permute-start.8 = (bf16[192,16,128]{2,1,0:T(8,128)(2,1)S(1)}, bf16[192,16,128]{2,1,0:T(8,128)(2,1)S(1)}, u32[]{:S(2)}, u32[]{:S(2)}) collective-permute-start(bf16[192,16,128]{2,1,0:T(8,128)(2,1)S(1)} %collective-permute-done.6.refs_8_.refs_9_), channel_id=1, source_target_pairs={{0,1},{1,0},{2,3},{3,2},{4,5},{5,4},{6,7},{7,6},{8,9},{9,8},{10,11... | collective-permute-start | bytes 2359304 | tf_op jit(solution)/shard_map/ppermute | solution.py:83
  84.9 0.7 copy-start.17
  85.6 11.6 %collective-permute-start.2 = (bf16[64,16,128]{2,1,0:T(8,128)(2,1)}, bf16[64,16,128]{2,1,0:T(8,128)(2,1)}, u32[]{:S(2)}, u32[]{:S(2)}) collective-permute-start(bf16[64,16,128]{2,1,0:T(8,128)(2,1)} %collective-permute-done.refs_4_.refs_5_), channel_id=1, source_target_pairs={{0,1},{1,0},{2,3},{3,2},{4,5},{5,4},{6,7},{7,6},{8,9},{9,8},{10,11... | collective-permute-start | bytes 786440 | tf_op jit(solution)/shard_map/ppermute | solution.py:83
  91.4 6.4 %collective-permute-start.13 = (bf16[128,8,128]{2,1,0:T(8,128)(2,1)}, bf16[128,8,128]{2,1,0:T(8,128)(2,1)}, u32[]{:S(2)}, u32[]{:S(2)}) collective-permute-start(bf16[128,8,128]{2,1,0:T(8,128)(2,1)} %collective-permute-done.11.refs_12_), channel_id=1, source_target_pairs={{0,1},{1,0},{2,3},{3,2},{4,5},{5,4},{6,7},{7,6},{8,9},{9,8},{10,11... | collective-permute-start | bytes 786440 | tf_op jit(solution)/shard_map/ppermute | solution.py:83
  97.2 1.9 %collective-permute-start.18 = (bf16[128,8,128]{2,1,0:T(8,128)(2,1)}, bf16[128,8,128]{2,1,0:T(8,128)(2,1)}, u32[]{:S(2)}, u32[]{:S(2)}) collective-permute-start(bf16[128,8,128]{2,1,0:T(8,128)(2,1)} %collective-permute-done.16.refs_16_), channel_id=1, source_target_pairs={{0,1},{1,0},{2,3},{3,2},{4,5},{5,4},{6,7},{7,6},{8,9},{9,8},{10,11... | collective-permute-start | bytes 786440 | tf_op jit(solution)/shard_map/ppermute | solution.py:83
  97.2 20.4 %collective-permute-start.27 = (bf16[128,8,128]{2,1,0:T(8,128)(2,1)}, bf16[128,8,128]{2,1,0:T(8,128)(2,1)}, u32[]{:S(2)}, u32[]{:S(2)}) collective-permute-start(bf16[128,8,128]{2,1,0:T(8,128)(2,1)} %copy-done.7), channel_id=1, source_target_pairs={{0,1},{1,0},{2,3},{3,2},{4,5},{5,4},{6,7},{7,6},{8,9},{9,8},{10,11... | collective-permute-start | bytes 786440 | tf_op jit(solution)/shard_map/ppermute | solution.py:83
  97.8 19.8 %collective-permute-start.22 = (bf16[128,8,128]{2,1,0:T(8,128)(2,1)}, bf16[128,8,128]{2,1,0:T(8,128)(2,1)}, u32[]{:S(2)}, u32[]{:S(2)}) collective-permute-start(bf16[128,8,128]{2,1,0:T(8,128)(2,1)} %copy-done.3), channel_id=1, source_target_pairs={{0,1},{1,0},{2,3},{3,2},{4,5},{5,4},{6,7},{7,6},{8,9},{9,8},{10,11... | collective-permute-start | bytes 786440 | tf_op jit(solution)/shard_map/ppermute | solution.py:83
  99.0 18.6 %collective-permute-start.28 = (bf16[128,8,128]{2,1,0:T(8,128)(2,1)}, bf16[128,8,128]{2,1,0:T(8,128)(2,1)}, u32[]{:S(2)}, u32[]{:S(2)}) collective-permute-start(bf16[128,8,128]{2,1,0:T(8,128)(2,1)} %copy-done.11), channel_id=1, source_target_pairs={{0,1},{1,0},{2,3},{3,2},{4,5},{5,4},{6,7},{7,6},{8,9},{9,8},{10,11... | collective-permute-start | bytes 786440 | tf_op jit(solution)/shard_map/ppermute | solution.py:83
  99.2 18.5 %collective-permute-start.23 = (bf16[128,8,128]{2,1,0:T(8,128)(2,1)}, bf16[128,8,128]{2,1,0:T(8,128)(2,1)}, u32[]{:S(2)}, u32[]{:S(2)}) collective-permute-start(bf16[128,8,128]{2,1,0:T(8,128)(2,1)} %copy-done.15), channel_id=1, source_target_pairs={{0,1},{1,0},{2,3},{3,2},{4,5},{5,4},{6,7},{7,6},{8,9},{9,8},{10,11... | collective-permute-start | bytes 786440 | tf_op jit(solution)/shard_map/ppermute | solution.py:83
  99.6 1.0 copy-start.1
  100.6 0.9 copy-start.6
  101.5 0.9 copy-start.10
  102.5 0.9 copy-start.14
  103.4 0.9 copy-start.18
  104.4 13.2 %copy-start.2 = (bf16[64,16,128]{2,1,0:T(8,128)(2,1)S(1)}, bf16[64,16,128]{2,1,0:T(8,128)(2,1)}, u32[]{:S(2)}) copy-start(bf16[64,16,128]{2,1,0:T(8,128)(2,1)} %copy-done) | copy-start | bytes 786436
  104.4 13.2 %copy-start.4 = (bf16[128,8,128]{2,1,0:T(8,128)(2,1)S(1)}, bf16[128,8,128]{2,1,0:T(8,128)(2,1)}, u32[]{:S(2)}) copy-start(bf16[128,8,128]{2,1,0:T(8,128)(2,1)} %copy-done.3) | copy-start | bytes 786436
  104.4 13.3 %copy-start.8 = (bf16[128,8,128]{2,1,0:T(8,128)(2,1)S(1)}, bf16[128,8,128]{2,1,0:T(8,128)(2,1)}, u32[]{:S(2)}) copy-start(bf16[128,8,128]{2,1,0:T(8,128)(2,1)} %copy-done.7) | copy-start | bytes 786436
  104.4 13.3 %copy-start.12 = (bf16[128,8,128]{2,1,0:T(8,128)(2,1)S(1)}, bf16[128,8,128]{2,1,0:T(8,128)(2,1)}, u32[]{:S(2)}) copy-start(bf16[128,8,128]{2,1,0:T(8,128)(2,1)} %copy-done.11) | copy-start | bytes 786436
  104.4 13.3 %copy-start.16 = (bf16[128,8,128]{2,1,0:T(8,128)(2,1)S(1)}, bf16[128,8,128]{2,1,0:T(8,128)(2,1)}, u32[]{:S(2)}) copy-start(bf16[128,8,128]{2,1,0:T(8,128)(2,1)} %copy-done.15) | copy-start | bytes 786436
  (3 other events, 2.1 us)
